TPU v7x, 32 devices: a whole 2x2x4 slice. The times are simulated.
32 devices in a mesh: batch: 4 (over x, core), centers: 8 (over z, y).
Axes of the slice: x: 2, y: 2, z: 4, core: 2. Of those that a mesh axis runs over, the one named last changes fastest.
Arguments:
- pool_features: float32 [32768, 128], P(('batch', 'centers')), may hold values from -14 to 14
- pool_targets: float32 [32768, 64], P(('batch', 'centers')), may hold values from -6 to 6
- batch_index: int32 [2048], P(('batch', 'centers')), may hold values from 0 to 1023
- centers: float32 [4096, 128], P('centers'), may hold values from -14 to 14
- weights: float32 [4096, 64], P('centers'), as said below
- eig_vectors: float32 [4096, 1024], P(('batch', 'centers')), may hold values from -0.09375 to 0.09375
- eig_scale: float32 [1024], replicated, may hold values from 0.5 to 4
- nys_owner: int32 [4096, 1], P(('batch', 'centers')), may hold values from 0 to 7; in each aligned block of 128 rows (0 to 127, 128 to 255, ...) at most 32 rows name the same one
- nys_offset: int32 [4096], P(('batch', 'centers')), may hold values from 0 to 511
Outputs:
- residual_out: float32 [2048, 64], P(('batch', 'centers'))
- update: float32 [4096, 64], P('centers')
Inputs may be any that keep to these rules, and one draw needn't show every extreme that they name: `nys_owner`: among the 128 rows of one device no owner is named more than 32 times; on some devices one owner is named exactly 32 times. `weights`: every column sums to zero.
All inputs are finite; a program needn't handle non-finite values.
Results may differ from a plain program's by a relative error of at most 0.0003.
Values sent between devices are 32-bit elements; how exact they have to be, the bound alone decides.
A program may use at most 64 MiB of HBM per device.

v0:
```python
import math
import jax
import jax.numpy as jnp
from jax import lax
from jax.sharding import PartitionSpec as P

DEPTH = 3
epsilon = 1e-06
highest = lax.Precision.HIGHEST


def kernel_rows(row_block, center_block, center_norm):
    inner_prod = (
        lax.dot_general(
            row_block,
            center_block,
            (((1,), (1,)), ((), ())),
            precision=highest,
            preferred_element_type=jnp.float32,
        )
        / row_block.shape[1]
    )
    row_norm = jnp.mean(row_block * row_block, axis=1) + epsilon
    norm_scale = jnp.sqrt(row_norm[:, None] * center_norm[None, :])
    sigma_now = inner_prod
    tangent = inner_prod
    for depth_step in range(DEPTH):
        cosine = sigma_now / norm_scale
        arc_angle = jnp.arccos(cosine)
        remain = (math.pi - arc_angle) / math.pi
        sigma_now = (
            norm_scale
            * (jnp.sqrt(1.0 - cosine * cosine) + (math.pi - arc_angle) * cosine)
            / math.pi
        )
        tangent = sigma_now + tangent * remain
    return tangent


def per_device(
    pool_features,
    pool_targets,
    batch_index,
    centers,
    weights,
    eig_vectors,
    eig_scale,
    nys_owner,
    nys_offset,
):
    local_rows = pool_features[batch_index]
    local_targets = pool_targets[batch_index]
    row_count = local_rows.shape[0]
    group_size = lax.axis_size("centers")
    rows_total = row_count * group_size * lax.axis_size("batch")
    center_count = centers.shape[0]
    outputs = weights.shape[1]
    center_norm = jnp.mean(centers * centers, axis=1) + epsilon
    kernel = kernel_rows(
        lax.all_gather(local_rows, "centers", axis=0, tiled=True), centers, center_norm
    )
    partial_pred = jnp.dot(kernel, weights, precision=highest, preferred_element_type=jnp.float32)
    all_targets = lax.all_gather(local_targets, "centers", axis=0, tiled=True)
    prediction = lax.psum(partial_pred, "centers")
    residual = prediction - all_targets
    own_residual = lax.dynamic_slice_in_dim(
        residual, lax.axis_index("centers") * row_count, row_count, 0
    )
    grads_part = lax.dot_general(
        kernel,
        residual,
        (((0,), (0,)), ((), ())),
        precision=highest,
        preferred_element_type=jnp.float32,
    ) / math.sqrt(rows_total)
    grads = lax.psum(grads_part, "batch")
    owner = nys_owner[:, 0]
    slots = max(2, 2 * owner.shape[0] // group_size)
    owner_hot = (owner[:, None] == jnp.arange(group_size, dtype=jnp.int32)[None, :]).astype(
        jnp.int32
    )
    slot_rank = jnp.sum((jnp.cumsum(owner_hot, axis=0) - owner_hot) * owner_hot, axis=1)
    requests = jnp.zeros((group_size, slots), jnp.int32).at[owner, slot_rank].set(nys_offset)
    received = lax.all_to_all(requests, "centers", split_axis=0, concat_axis=0, tiled=True)
    found = grads[received]
    returned = lax.all_to_all(found, "centers", split_axis=0, concat_axis=0, tiled=True)
    picked_grads = returned[owner, slot_rank]
    coeff_part = lax.dot_general(
        eig_vectors,
        picked_grads,
        (((0,), (0,)), ((), ())),
        precision=highest,
        preferred_element_type=jnp.float32,
    )
    coeff = lax.psum(coeff_part, ("batch", "centers"))
    corr_rows = jnp.dot(
        eig_vectors,
        eig_scale[:, None] * coeff,
        precision=highest,
        preferred_element_type=jnp.float32,
    )
    outgoing = (
        jnp.zeros((group_size, slots, outputs), jnp.float32).at[owner, slot_rank].set(corr_rows)
    )
    incoming = lax.all_to_all(outgoing, "centers", split_axis=0, concat_axis=0, tiled=True)
    corr_part = jnp.zeros((center_count, outputs), jnp.float32).at[received].add(incoming)
    correction = lax.psum(corr_part, "batch")
    return (own_residual, correction - grads)


def solution(mesh):
    placed = (
        P(("batch", "centers"), None),
        P(("batch", "centers"), None),
        P(("batch", "centers")),
        P("centers", None),
        P("centers", None),
        P(("batch", "centers"), None),
        P(),
        P(("batch", "centers"), None),
        P(("batch", "centers")),
    )
    return jax.shard_map(
        per_device,
        mesh=mesh,
        in_specs=placed,
        out_specs=(P(("batch", "centers"), None), P("centers", None)),
        check_vma=False,
    )
```

profile of v0, /device:TPU:0, one launch (start us, length us, event | category | flops | bytes accessed | tf_op | source)
XLA Modules:
  0.0 387.0 jit_solution(5106888059048131326)
XLA Ops:
  9.0 19.9 %scatter_fusion = s32[8,32]{1,0:T(8,128)} fusion(s32[8,32]{1,0:T(8,128)} %broadcast.104, s32[128]{0:T(128)S(1)} %get-tuple-element.8, s32[128]{0:T(128)S(1)} %copy-done.8), kind=kCustom, calls=%fused_computation.4 | custom fusion | bytes 2560 | tf_op jit(solution)/shard_map/scatter | solution.py:83
  28.9 7.4 %all-to-all-start = ((s32[8,1,32]{2,1,0:T(1,128)}), s32[8,1,32]{2,1,0:T(1,128)S(1)}, u32[]{:S(2)}, u32[]{:S(2)}) async-start(s32[8,1,32]{2,1,0:T(1,128)} %bitcast.4), calls=%async_computation | async-start | bytes 8192 | tf_op jit(solution)/shard_map/all_to_all | solution.py:84
  37.2 31.2 %all-gather = f32[512,128]{1,0:T(8,128)S(1)} all-gather(f32[64,128]{1,0:T(8,128)S(1)} %gather_fusion), channel_id=2, replica_groups=mesh['batch'=4,'centers'=8] {'centers'}, dimensions={0}, use_global_device_ids=true | all-gather | bytes 294912 | tf_op jit(solution)/shard_map/all_gather | solution.py:60
  68.6 8.9 %multiply_add_fusion = f32[512,512]{1,0:T(8,128)S(1)} fusion(f32[512,128]{1,0:T(8,128)S(1)} %all-gather, f32[512,128]{1,0:T(8,128)S(1)} %copy-done.3, f32[512]{0:T(512)S(1)} %multiply_add_fusion.1, f32[512]{0:T(512)S(1)} %multiply_add_fusion.2), kind=kOutput, calls=%fused_computation.11 | convolution fusion | flops 414187520 | bytes 1576960 | tf_op jit(solution)/shard_map/dot_general | solution.py:14
  77.5 1.8 fusion.8
  80.2 30.8 %all-gather.1 = f32[512,64]{1,0:T(8,128)S(1)} all-gather(f32[64,64]{1,0:T(8,128)S(1)} %gather_fusion.1), channel_id=3, replica_groups=mesh['batch'=4,'centers'=8] {'centers'}, dimensions={0}, use_global_device_ids=true | all-gather | bytes 147456 | tf_op jit(solution)/shard_map/all_gather | solution.py:63
  111.3 39.5 %all-reduce.5.cloned.1.call-done = f32[512,64]{0,1:T(8,128)} async-done(((f32[512,64]{0,1:T(8,128)}), f32[512,64]{0,1:T(8,128)}) %all-reduce.5.cloned.1.call-update) | async-done | bytes 131088 | tf_op jit(solution)/shard_map/psum | solution.py:64
  150.8 0.9 sub.36
  151.7 1.5 convolution_multiply_fusion.1
  153.3 31.3 %all-reduce.7.cloned.1.call-done = f32[512,64]{0,1:T(8,128)} async-done(((f32[512,64]{0,1:T(8,128)}), f32[512,64]{0,1:T(8,128)}) %all-reduce.7.cloned.1.call-update) | async-done | bytes 131088 | tf_op jit(solution)/shard_map/psum | solution.py:76
  184.6 1.0 copy.26
  186.5 12.2 %all_to_all.22 = f32[8,1,2048]{2,1,0:T(1,128)S(1)} all-to-all(f32[8,1,2048]{2,1,0:T(1,128)S(1)} %reshape.114), channel_id=1, replica_groups=mesh['batch'=4,'centers'=8] {'centers'}, dimensions={0} | all-to-all | bytes 131072 | tf_op jit(solution)/shard_map/all_to_all | solution.py:86
  199.2 0.8 reduce
  200.1 1.2 gather_fusion.3
  201.3 1.1 convolution_bitcast_fusion
  202.5 123.4 %all-reduce.9.cloned.1.call-done = f32[1024,64]{0,1:T(8,128)} async-done(((f32[1024,64]{0,1:T(8,128)}), f32[1024,64]{0,1:T(8,128)}) %all-reduce.9.cloned.1.call-update) | async-done | bytes 262160 | tf_op jit(solution)/shard_map/psum | solution.py:95
  325.9 1.6 convolution_bitcast_fusion.1
  327.7 6.9 %scatter_fusion.1 = f32[8,32,64]{2,1,0:T(8,128)S(1)} fusion(f32[8,32,64]{2,1,0:T(8,128)S(1)} %broadcast_in_dim.8, s32[128]{0:T(128)S(1)} %get-tuple-element.8, f32[128,64]{1,0:T(8,128)S(1)} %copy.27), kind=kCustom, calls=%fused_computation.5 | custom fusion | bytes 99328 | tf_op jit(solution)/shard_map/scatter | solution.py:103
  335.3 4.5 %all-to-all-start.2 = ((f32[8,1,2048]{2,1,0:T(1,128)}), f32[8,1,2048]{2,1,0:T(1,128)S(1)}, u32[]{:S(2)}, u32[]{:S(2)}) async-start(f32[8,1,2048]{2,1,0:T(1,128)} %reshape.116), calls=%async_computation.2 | async-start | bytes 131072 | tf_op jit(solution)/shard_map/all_to_all | solution.py:105
  339.9 6.9 %all-to-all-done.2 = f32[8,1,2048]{2,1,0:T(1,128)S(1)} async-done(((f32[8,1,2048]{2,1,0:T(1,128)}), f32[8,1,2048]{2,1,0:T(1,128)S(1)}, u32[]{:S(2)}, u32[]{:S(2)}) %all-to-all-start.2) | async-done | bytes 65568 | tf_op jit(solution)/shard_map/all_to_all | solution.py:105
  346.7 0.8 reduce.1
  347.6 1.7 scatter_custom_fusion.2
  351.0 27.9 %all-reduce.11.cloned.1.call-done = f32[512,64]{0,1:T(8,128)} async-done(((f32[512,64]{0,1:T(8,128)}), f32[512,64]{0,1:T(8,128)}) %all-reduce.11.cloned.1.call-update) | async-done | bytes 131088 | tf_op jit(solution)/shard_map/psum | solution.py:107
  378.9 1.6 sub.38
  (58 shorter events, 7.9 us)
Async XLA Ops:
  7.2 194.2 %copy-start = (f32[128,1024]{1,0:T(8,128)S(1)}, f32[128,1024]{1,0:T(8,128)}, u32[]{:S(2)}) copy-start(f32[128,1024]{1,0:T(8,128)} %param.14) | copy-start | bytes 1572868
  7.2 0.7 copy-start.6
  8.3 0.7 copy-start.8
  9.0 27.4 %copy-start.3 = (f32[512,128]{1,0:T(8,128)S(1)}, f32[512,128]{1,0:T(8,128)}, u32[]{:S(2)}) copy-start(f32[512,128]{1,0:T(8,128)} %param.12) | copy-start | bytes 786436
  9.0 27.6 %copy-start.5 = (f32[1024,128]{1,0:T(8,128)S(1)}, f32[1024,128]{1,0:T(8,128)}, u32[]{:S(2)}) copy-start(f32[1024,128]{1,0:T(8,128)} %param.9) | copy-start | bytes 1572868
  28.9 7.5 %copy-start.9 = (s32[64]{0:T(128)S(1)}, s32[64]{0:T(128)}, u32[]{:S(2)}) copy-start(s32[64]{0:T(128)} %param.11) | copy-start | bytes 772
  28.9 82.3 %all-to-all-start = ((s32[8,1,32]{2,1,0:T(1,128)}), s32[8,1,32]{2,1,0:T(1,128)S(1)}, u32[]{:S(2)}, u32[]{:S(2)}) async-start(s32[8,1,32]{2,1,0:T(1,128)} %bitcast.4), calls=%async_computation | async-start | bytes 8192 | tf_op jit(solution)/shard_map/all_to_all | solution.py:84
  36.3 114.5 %all-reduce.5.cloned.1.call-start = ((), (), s32[]{:S(2)}) async-start(), calls=%async_computation.3 | async-start | bytes 262144 | tf_op jit(solution)/shard_map/psum | solution.py:64
  68.6 8.9 %copy-start.4 = (f32[512,64]{0,1:T(8,128)S(1)}, f32[512,64]{0,1:T(8,128)}, u32[]{:S(2)}) copy-start(f32[512,64]{0,1:T(8,128)} %param.13) | copy-start | bytes 393220
  77.5 1.9 copy-start.2
  79.4 105.2 %all-reduce.7.cloned.1.call-start = ((), (), s32[]{:S(2)}) async-start(), calls=%async_computation.4 | async-start | bytes 262144 | tf_op jit(solution)/shard_map/psum | solution.py:76
  153.2 172.7 %all-reduce.9.cloned.1.call-start = ((), (), s32[]{:S(2)}) async-start(), calls=%async_computation.5 | async-start | bytes 524288 | tf_op jit(solution)/shard_map/psum | solution.py:95
  202.5 123.4 %copy-start.7 = (f32[1024]{0:T(1024)S(1)}, f32[1024]{0:T(1024)}, u32[]{:S(2)}) copy-start(f32[1024]{0:T(1024)} %param.15) | copy-start | bytes 12292
  335.3 11.4 %all-to-all-start.2 = ((f32[8,1,2048]{2,1,0:T(1,128)}), f32[8,1,2048]{2,1,0:T(1,128)S(1)}, u32[]{:S(2)}, u32[]{:S(2)}) async-start(f32[8,1,2048]{2,1,0:T(1,128)} %reshape.116), calls=%async_computation.2 | async-start | bytes 131072 | tf_op jit(solution)/shard_map/all_to_all | solution.py:105
  339.8 39.0 %all-reduce.11.cloned.1.call-start = ((), (), s32[]{:S(2)}) async-start(), calls=%async_computation.6 | async-start | bytes 262144 | tf_op jit(solution)/shard_map/psum | solution.py:107
  350.1 28.7 %copy-start.1 = (f32[512,64]{0,1:T(8,128)S(1)}, f32[512,64]{0,1:T(8,128)}, u32[]{:S(2)}) copy-start(f32[512,64]{0,1:T(8,128)} %all-reduce.7.cloned.1.call-done) | copy-start | bytes 393220
Sparse Core Ops, SparseCore 0:
  79.5 71.2 all-reduce.4
  153.7 30.8 all-reduce.6
  202.6 123.2 all-reduce.8
  350.3 28.5 all-reduce.10
where the time goes:
time: 388 us; the launch traced here: 387 us
  waiting for transfers between devices  229 us (59%)
  blocking collectives  74.3 us (19%)
  local copies, waits for them, and re-layouts  36 us (9%)
  matrix products  14.9 us (4%)
  between operations  14 us (4%)
  starting transfers between devices  12.1 us (3%)
  other arithmetic  6.6 us (2%)
    psum x1, waiting for transfers between devices, per_device(): coeff = lax.psum(coeff_part, ('batch', 'centers'))  123 us
    psum x1, waiting for transfers between devices, per_device(): prediction = lax.psum(partial_pred, 'centers')  39.5 us
    psum x1, waiting for transfers between devices, per_device(): grads = lax.psum(grads_part, 'batch')  31.3 us
    all_gather x1, blocking collectives, per_device(): lax.all_gather(local_rows, 'centers', axis=0, tiled=True)  31.2 us
    all_gather x1, blocking collectives, per_device(): all_targets = lax.all_gather(local_targets, 'centers', axis=0, tiled=True)  30.8 us
    psum x1, waiting for transfers between devices, per_device(): correction = lax.psum(corr_part, 'batch')  27.9 us
    scatter x1, local copies, waits for them, and re-layouts, per_device(): jnp.zeros((group_size, slots), jnp.int32).at[owner, slot_rank]  19.9 us
    all_to_all x1, blocking collectives, per_device(): lax.all_to_all(found, 'centers', split_axis=0, concat_axis=0, tiled=True)  12.2 us
  transfers between devices with their start and end apart: 6, of which 5 were waited for; matrix products, arithmetic and copies ran while one was open for 3% of the time, Pallas kernels for 0%

commit v1 on v0

--- a/solution.py
+++ b/solution.py
@@ -1,3 +1,4 @@
+import functools
 import math
 import jax
 import jax.numpy as jnp
@@ -7,6 +8,13 @@
 DEPTH = 3
 epsilon = 1e-06
 highest = lax.Precision.HIGHEST
+
+
+def ends_read(tile_in, comm_axis, net_axis):
+    return lax.psum(lax.psum(tile_in, axis_name=comm_axis), axis_name=net_axis)
+
+
+_lead_terms = functools.partial(ends_read, comm_axis="batch", net_axis="centers")
 
 
 def kernel_rows(row_block, center_block, center_norm):
@@ -92,7 +100,7 @@
         precision=highest,
         preferred_element_type=jnp.float32,
     )
-    coeff = lax.psum(coeff_part, ("batch", "centers"))
+    coeff = _lead_terms(coeff_part)
     corr_rows = jnp.dot(
         eig_vectors,
         eig_scale[:, None] * coeff,

time: 388 us -> 368 us (0.948)
  waiting for transfers between devices: 229 us -> 210 us
    psum x1 -> x2, waiting for transfers between devices: 123 us -> 103 us  [ends_read(): return lax.psum(lax.psum(tile_in, axis_name=comm_axis), axis_name=net_axis)]
  transfers between devices with their start and end apart: 6 -> 7, of which waited for: 5 -> 6; matrix products, arithmetic and copies ran while one was open for 3% -> 4% of each run, Pallas kernels for 0% -> 0%
where the time goes in v1:
time: 368 us; the launch traced here: 367 us
  waiting for transfers between devices  210 us (57%)
  blocking collectives  74.3 us (20%)
  local copies, waits for them, and re-layouts  36 us (10%)
  matrix products  14.9 us (4%)
  between operations  14 us (4%)
  starting transfers between devices  11.4 us (3%)
  other arithmetic  6.6 us (2%)
    psum x2, waiting for transfers between devices, ends_read(): return lax.psum(lax.psum(tile_in, axis_name=comm_axis), axis_name=net_axis)  103 us
    psum x1, waiting for transfers between devices, per_device(): prediction = lax.psum(partial_pred, 'centers')  39.5 us
    psum x1, waiting for transfers between devices, per_device(): grads = lax.psum(grads_part, 'batch')  31.3 us
    all_gather x1, blocking collectives, per_device(): lax.all_gather(local_rows, 'centers', axis=0, tiled=True)  31.2 us
    all_gather x1, blocking collectives, per_device(): all_targets = lax.all_gather(local_targets, 'centers', axis=0, tiled=True)  30.8 us
    psum x1, waiting for transfers between devices, per_device(): correction = lax.psum(corr_part, 'batch')  28.8 us
    scatter x1, local copies, waits for them, and re-layouts, per_device(): jnp.zeros((group_size, slots), jnp.int32).at[owner, slot_rank]  19.9 us
    all_to_all x1, blocking collectives, per_device(): lax.all_to_all(found, 'centers', split_axis=0, concat_axis=0, tiled=True)  12.2 us
  transfers between devices with their start and end apart: 7, of which 6 were waited for; matrix products, arithmetic and copies ran while one was open for 4% of the time, Pallas kernels for 0%

profile of v1, /device:TPU:0, one launch (start us, length us, event | category | flops | bytes accessed | tf_op | source)
XLA Modules:
  0.0 367.0 jit_solution(14997561860119243724)
XLA Ops:
  9.0 19.9 %scatter_fusion = s32[8,32]{1,0:T(8,128)} fusion(s32[8,32]{1,0:T(8,128)} %broadcast.104, s32[128]{0:T(128)S(1)} %get-tuple-element.8, s32[128]{0:T(128)S(1)} %copy-done.8), kind=kCustom, calls=%fused_computation.4 | custom fusion | bytes 2560 | tf_op jit(solution)/shard_map/scatter | solution.py:91
  28.9 7.4 %all-to-all-start = ((s32[8,1,32]{2,1,0:T(1,128)}), s32[8,1,32]{2,1,0:T(1,128)S(1)}, u32[]{:S(2)}, u32[]{:S(2)}) async-start(s32[8,1,32]{2,1,0:T(1,128)} %bitcast.4), calls=%async_computation | async-start | bytes 8192 | tf_op jit(solution)/shard_map/all_to_all | solution.py:92
  37.2 31.2 %all-gather = f32[512,128]{1,0:T(8,128)S(1)} all-gather(f32[64,128]{1,0:T(8,128)S(1)} %gather_fusion), channel_id=2, replica_groups=mesh['batch'=4,'centers'=8] {'centers'}, dimensions={0}, use_global_device_ids=true | all-gather | bytes 294912 | tf_op jit(solution)/shard_map/all_gather | solution.py:68
  68.6 8.9 %multiply_add_fusion = f32[512,512]{1,0:T(8,128)S(1)} fusion(f32[512,128]{1,0:T(8,128)S(1)} %all-gather, f32[512,128]{1,0:T(8,128)S(1)} %copy-done.3, f32[512]{0:T(512)S(1)} %multiply_add_fusion.1, f32[512]{0:T(512)S(1)} %multiply_add_fusion.2), kind=kOutput, calls=%fused_computation.11 | convolution fusion | flops 414187520 | bytes 1576960 | tf_op jit(solution)/shard_map/dot_general | solution.py:22
  77.5 1.8 fusion.8
  80.2 30.8 %all-gather.1 = f32[512,64]{1,0:T(8,128)S(1)} all-gather(f32[64,64]{1,0:T(8,128)S(1)} %gather_fusion.1), channel_id=3, replica_groups=mesh['batch'=4,'centers'=8] {'centers'}, dimensions={0}, use_global_device_ids=true | all-gather | bytes 147456 | tf_op jit(solution)/shard_map/all_gather | solution.py:71
  111.3 39.5 %all-reduce.6.cloned.1.call-done = f32[512,64]{0,1:T(8,128)} async-done(((f32[512,64]{0,1:T(8,128)}), f32[512,64]{0,1:T(8,128)}) %all-reduce.6.cloned.1.call-update) | async-done | bytes 131088 | tf_op jit(solution)/shard_map/psum | solution.py:72
  150.8 0.9 sub.36
  151.7 1.5 convolution_multiply_fusion.1
  153.3 31.3 %all-reduce.8.cloned.1.call-done = f32[512,64]{0,1:T(8,128)} async-done(((f32[512,64]{0,1:T(8,128)}), f32[512,64]{0,1:T(8,128)}) %all-reduce.8.cloned.1.call-update) | async-done | bytes 131088 | tf_op jit(solution)/shard_map/psum | solution.py:84
  184.6 1.0 copy.26
  186.5 12.2 %all_to_all.22 = f32[8,1,2048]{2,1,0:T(1,128)S(1)} all-to-all(f32[8,1,2048]{2,1,0:T(1,128)S(1)} %reshape.114), channel_id=1, replica_groups=mesh['batch'=4,'centers'=8] {'centers'}, dimensions={0} | all-to-all | bytes 131072 | tf_op jit(solution)/shard_map/all_to_all | solution.py:94
  199.2 0.8 reduce
  200.1 1.2 gather_fusion.3
  201.3 1.1 convolution_bitcast_fusion
  202.5 29.0 %all-reduce.10.cloned.1.call-done = f32[1024,64]{0,1:T(8,128)} async-done(((f32[1024,64]{0,1:T(8,128)}), f32[1024,64]{0,1:T(8,128)}) %all-reduce.10.cloned.1.call-update) | async-done | bytes 262160 | tf_op jit(solution)/shard_map/psum | solution.py:14
  231.5 74.2 %all-reduce.12.cloned.1.call-done = f32[1024,64]{0,1:T(8,128)} async-done(((f32[1024,64]{0,1:T(8,128)}), f32[1024,64]{0,1:T(8,128)}) %all-reduce.12.cloned.1.call-update) | async-done | bytes 262160 | tf_op jit(solution)/shard_map/psum | solution.py:14
  305.8 1.6 convolution_bitcast_fusion.1
  307.5 6.9 %scatter_fusion.1 = f32[8,32,64]{2,1,0:T(8,128)S(1)} fusion(f32[8,32,64]{2,1,0:T(8,128)S(1)} %broadcast_in_dim.8, s32[128]{0:T(128)S(1)} %get-tuple-element.8, f32[128,64]{1,0:T(8,128)S(1)} %copy.27), kind=kCustom, calls=%fused_computation.5 | custom fusion | bytes 99328 | tf_op jit(solution)/shard_map/scatter | solution.py:111
  315.2 3.8 %all-to-all-start.2 = ((f32[8,1,2048]{2,1,0:T(1,128)}), f32[8,1,2048]{2,1,0:T(1,128)S(1)}, u32[]{:S(2)}, u32[]{:S(2)}) async-start(f32[8,1,2048]{2,1,0:T(1,128)} %reshape.116), calls=%async_computation.2 | async-start | bytes 131072 | tf_op jit(solution)/shard_map/all_to_all | solution.py:113
  319.0 6.9 %all-to-all-done.2 = f32[8,1,2048]{2,1,0:T(1,128)S(1)} async-done(((f32[8,1,2048]{2,1,0:T(1,128)}), f32[8,1,2048]{2,1,0:T(1,128)S(1)}, u32[]{:S(2)}, u32[]{:S(2)}) %all-to-all-start.2) | async-done | bytes 65568 | tf_op jit(solution)/shard_map/all_to_all | solution.py:113
  326.8 1.7 scatter_custom_fusion.2
  330.1 28.8 %all-reduce.14.cloned.1.call-done = f32[512,64]{0,1:T(8,128)} async-done(((f32[512,64]{0,1:T(8,128)}), f32[512,64]{0,1:T(8,128)}) %all-reduce.14.cloned.1.call-update) | async-done | bytes 131088 | tf_op jit(solution)/shard_map/psum | solution.py:115
  358.9 1.6 sub.38
  (61 shorter events, 8.8 us)
Async XLA Ops:
  7.2 194.2 %copy-start = (f32[128,1024]{1,0:T(8,128)S(1)}, f32[128,1024]{1,0:T(8,128)}, u32[]{:S(2)}) copy-start(f32[128,1024]{1,0:T(8,128)} %param.14) | copy-start | bytes 1572868
  7.2 0.7 copy-start.6
  8.3 0.7 copy-start.8
  9.0 27.4 %copy-start.3 = (f32[512,128]{1,0:T(8,128)S(1)}, f32[512,128]{1,0:T(8,128)}, u32[]{:S(2)}) copy-start(f32[512,128]{1,0:T(8,128)} %param.12) | copy-start | bytes 786436
  9.0 27.6 %copy-start.5 = (f32[1024,128]{1,0:T(8,128)S(1)}, f32[1024,128]{1,0:T(8,128)}, u32[]{:S(2)}) copy-start(f32[1024,128]{1,0:T(8,128)} %param.9) | copy-start | bytes 1572868
  28.9 7.5 %copy-start.9 = (s32[64]{0:T(128)S(1)}, s32[64]{0:T(128)}, u32[]{:S(2)}) copy-start(s32[64]{0:T(128)} %param.11) | copy-start | bytes 772
  28.9 82.3 %all-to-all-start = ((s32[8,1,32]{2,1,0:T(1,128)}), s32[8,1,32]{2,1,0:T(1,128)S(1)}, u32[]{:S(2)}, u32[]{:S(2)}) async-start(s32[8,1,32]{2,1,0:T(1,128)} %bitcast.4), calls=%async_computation | async-start | bytes 8192 | tf_op jit(solution)/shard_map/all_to_all | solution.py:92
  36.3 114.5 %all-reduce.6.cloned.1.call-start = ((), (), s32[]{:S(2)}) async-start(), calls=%async_computation.3 | async-start | bytes 262144 | tf_op jit(solution)/shard_map/psum | solution.py:72
  68.6 8.9 %copy-start.4 = (f32[512,64]{0,1:T(8,128)S(1)}, f32[512,64]{0,1:T(8,128)}, u32[]{:S(2)}) copy-start(f32[512,64]{0,1:T(8,128)} %param.13) | copy-start | bytes 393220
  77.5 1.9 copy-start.2
  79.4 105.2 %all-reduce.8.cloned.1.call-start = ((), (), s32[]{:S(2)}) async-start(), calls=%async_computation.4 | async-start | bytes 262144 | tf_op jit(solution)/shard_map/psum | solution.py:84
  153.2 78.3 %all-reduce.10.cloned.1.call-start = ((), (), s32[]{:S(2)}) async-start(), calls=%async_computation.5 | async-start | bytes 524288 | tf_op jit(solution)/shard_map/psum | solution.py:14
  202.5 103.3 %all-reduce.12.cloned.1.call-start = ((), (), s32[]{:S(2)}) async-start(), calls=%async_computation.6 | async-start | bytes 524288 | tf_op jit(solution)/shard_map/psum | solution.py:14
  231.5 74.3 %copy-start.7 = (f32[1024]{0:T(1024)S(1)}, f32[1024]{0:T(1024)}, u32[]{:S(2)}) copy-start(f32[1024]{0:T(1024)} %param.15) | copy-start | bytes 12292
  315.2 10.7 %all-to-all-start.2 = ((f32[8,1,2048]{2,1,0:T(1,128)}), f32[8,1,2048]{2,1,0:T(1,128)S(1)}, u32[]{:S(2)}, u32[]{:S(2)}) async-start(f32[8,1,2048]{2,1,0:T(1,128)} %reshape.116), calls=%async_computation.2 | async-start | bytes 131072 | tf_op jit(solution)/shard_map/all_to_all | solution.py:113
  319.0 39.9 %all-reduce.14.cloned.1.call-start = ((), (), s32[]{:S(2)}) async-start(), calls=%async_computation.7 | async-start | bytes 262144 | tf_op jit(solution)/shard_map/psum | solution.py:115
  329.3 29.6 %copy-start.1 = (f32[512,64]{0,1:T(8,128)S(1)}, f32[512,64]{0,1:T(8,128)}, u32[]{:S(2)}) copy-start(f32[512,64]{0,1:T(8,128)} %all-reduce.8.cloned.1.call-done) | copy-start | bytes 393220
Sparse Core Ops, SparseCore 0:
  79.5 71.2 all-reduce.5
  153.7 30.8 all-reduce.7
  202.6 28.8 all-reduce.9
  234.7 71.0 all-reduce.11
  329.4 29.3 all-reduce.13
